TPU v7x, 32 devices: a whole 2x2x4 slice. The times are simulated.
32 devices in a mesh: grp: 2 (over y), ka: 4 (over z), ga: 2 (over x), ba: 2 (over core).
Axes of the slice: x: 2, y: 2, z: 4, core: 2. Of those that a mesh axis runs over, the one named last changes fastest.
Arguments:
- coefficients: bfloat16 [2, 2, 16, 512, 9216], P(None, None, ('grp', 'ka'), 'ba', 'ga'), parts along dimension 2, may hold values from -1 to 1
- occupied: int32 [2, 16], P(None, ('grp', 'ka')), parts along dimension 1, may hold values from 64 to 512
- kweights: float32 [16], P(('grp', 'ka')), parts along dimension 0, may hold values from 0.5 to 2
- owner_map: int32 [1024], P('grp'), parts along dimension 0, may hold values from 0 to 7, as said below
- species: int32 [1024], P('grp'), parts along dimension 0, may hold values from 0 to 1
- positions: float32 [3, 1024], P(None, 'grp'), parts along dimension 1, may hold values from 0 to 100
- multipole: float32 [2, 9, 324], replicated, may hold values from -0.3125 to 0.3125
- widths: float32 [2], replicated, may hold values from 0.05 to 0.3
- potential: float32 [2, 442368], P(None, ('grp', 'ga')), parts along dimension 1, may hold values from -0.013671875 to 0.013671875
Outputs:
- density: float32 [2, 2, 1024, 324], P(None, None, ('grp', 'ka', 'ga', 'ba')), parts along dimension 2
- forces: float32 [3, 1024], P(None, ('grp', 'ka', 'ga', 'ba')), parts along dimension 1
There are 2 independent parts, one for each index of `grp`. A program takes and returns all parts, laid end to end along the dimension named above; an argument that names none is the same for every part. Nothing has to cross between parts.
Inputs may be any that keep to these rules, and one draw needn't show every extreme that they name: `owner_map`: within each aligned block of 256 atoms every owner number is named by exactly 32 atoms.
All inputs are finite; a program needn't handle non-finite values.
Results may differ from a plain program's by a relative error of at most 0.0003.
Values sent between devices are 32-bit elements; how exact they have to be, the bound alone decides.
A program may use at most 192 MiB of HBM per device.

v0:
```python
import jax
import jax.numpy as jnp
from jax import lax
from jax.sharding import PartitionSpec as P

NPROJ = 18
SPECIES = 2
NL = 9
GRID = 96
grid_step = 0.0625
highest = lax.Precision.HIGHEST


def harmonics(start_index, length, widths):
    indices = start_index + jnp.arange(length, dtype=jnp.int32)
    planes = [indices % GRID, indices // GRID % GRID, indices // (GRID * GRID)]
    vectors = []
    for plane_index in planes:
        signed = jnp.where(plane_index >= GRID // 2, plane_index - GRID, plane_index)
        vectors.append(grid_step * signed.astype(jnp.float32))
    along_x, along_y, along_z = vectors
    square = along_x * along_x + along_y * along_y + along_z * along_z
    shapes = jnp.stack(
        [
            jnp.ones_like(square),
            along_x,
            along_y,
            along_z,
            along_x * along_y,
            along_y * along_z,
            along_z * along_x,
            along_x * along_x - along_y * along_y,
            3.0 * along_z * along_z - square,
        ]
    )
    damping = jnp.exp(-widths[:, None] * square[None, :])
    form_table = (damping[:, None, :] * shapes[None, :, :]).reshape(SPECIES * NL, length)
    return (form_table, jnp.stack(vectors, axis=1))


def force_block(moments, places, form_table, vectors, pot_piece):
    smooth = jnp.dot(moments, form_table, precision=highest)
    phases = jnp.dot(places, vectors.T, precision=highest)
    wave_term = pot_piece[0][None, :] * jnp.sin(phases) + pot_piece[1][None, :] * jnp.cos(phases)
    return jnp.dot(smooth * wave_term, vectors, precision=highest)


def local_force(moments, places, pot_piece, start_index, widths):
    length = pot_piece.shape[1]
    pieces = 8
    width_block = length // pieces

    def gblock(running, number):
        offset = number * width_block
        form_table, vectors = harmonics(start_index + offset, width_block, widths)
        segment = lax.dynamic_slice_in_dim(pot_piece, offset, width_block, 1)
        return (running + force_block(moments, places, form_table, vectors, segment), None)

    result, unused = lax.scan(
        gblock, jnp.zeros((moments.shape[0], 3), jnp.float32), jnp.arange(pieces, dtype=jnp.int32)
    )
    return result


def shards(
    coefficients, occupied, kweights, owner_map, species, positions, multipole, widths, potential
):
    spin_count, complex_parts, kcount, bcount, columns = coefficients.shape
    atoms_blk = columns // NPROJ
    kgroups = lax.axis_size("ka")
    bgroups = lax.axis_size("ba")
    owners = kgroups * bgroups
    per_owner = atoms_blk // owners
    owner_index = lax.axis_index(("ka", "ba"))
    group_index = lax.axis_index("ga")
    band_index = lax.axis_index("ba") * bcount + jnp.arange(bcount, dtype=jnp.int32)
    band_mask = (band_index[None, None, :] < occupied[:, :, None]).astype(jnp.bfloat16)
    values = coefficients.reshape(spin_count, complex_parts, kcount, bcount, atoms_blk, NPROJ)
    masked = values * band_mask[:, None, :, :, None, None]
    real_part = jnp.einsum(
        "sckbai,sckbaj->skaij", values, masked, preferred_element_type=jnp.float32
    )
    cross_term = jnp.einsum(
        "skbai,skbaj->skaij", values[:, 0], masked[:, 1], preferred_element_type=jnp.float32
    )
    imag_part = cross_term - jnp.swapaxes(cross_term, 3, 4)
    weighted = jnp.stack([real_part, imag_part], axis=1) * kweights[None, None, :, None, None, None]
    density_local = jnp.sum(weighted, axis=2).reshape(
        spin_count, complex_parts, atoms_blk, NPROJ * NPROJ
    )
    ranking = jnp.argsort(owner_map.reshape(-1, atoms_blk), axis=1, stable=True)
    own_ranks = lax.dynamic_slice_in_dim(ranking, owner_index * per_owner, per_owner, 1)
    summed = lax.psum(density_local, ("ka", "ba"))
    own_rows = lax.dynamic_index_in_dim(own_ranks, group_index, 0, keepdims=False)
    own_density = jnp.take(summed, own_rows, axis=2)
    block_count = own_ranks.shape[0]
    atom_ids = jnp.arange(block_count, dtype=jnp.int32)[:, None] * atoms_blk + own_ranks
    own_atoms = lax.dynamic_index_in_dim(atom_ids, group_index, 0, keepdims=False)
    real_total = jnp.sum(own_density[:, 0], axis=0)
    selector = (
        jnp.take(species, own_atoms)[:, None] == jnp.arange(SPECIES, dtype=jnp.int32)[None, :]
    ).astype(jnp.float32)
    moments = jnp.dot(
        real_total, multipole.reshape(SPECIES * NL, NPROJ * NPROJ).T, precision=highest
    ) * jnp.repeat(selector, NL, axis=1)
    gcount = potential.shape[1]
    all_moments = lax.all_gather(moments, "ga", axis=0, tiled=True)
    places = jnp.take(positions, atom_ids.reshape(-1), axis=1).T
    partial_force = local_force(all_moments, places, potential, group_index * gcount, widths)
    summed_force = lax.psum(partial_force, "ga")
    own_force = lax.dynamic_slice_in_dim(summed_force, group_index * per_owner, per_owner, 0)
    return (own_density, own_force.T)


def solution(mesh):
    placed = (
        P(None, None, ("grp", "ka"), "ba", "ga"),
        P(None, ("grp", "ka")),
        P(("grp", "ka")),
        P("grp"),
        P("grp"),
        P(None, "grp"),
        P(),
        P(),
        P(None, ("grp", "ga")),
    )
    return jax.shard_map(
        shards,
        mesh=mesh,
        in_specs=placed,
        out_specs=(
            P(None, None, ("grp", "ka", "ga", "ba"), None),
            P(None, ("grp", "ka", "ga", "ba")),
        ),
        check_vma=False,
    )
```

profile of v0, /device:TPU:0, one launch (start us, length us, event | category | flops | bytes accessed | tf_op | source)
XLA Modules:
  0.0 663.2 jit_solution(12733213700706561287)
XLA Ops:
  10.0 45.7 %copy.45 = bf16[2,2,2,256,4608]{3,2,4,1,0:T(2,128)(2,1)} copy(bf16[2,2,2,256,4608]{4,3,2,1,0:T(8,128)(2,1)} %param.11) | data formatting | bytes 37748736 | tf_op args[0]
  55.7 45.4 %copy.46 = bf16[2,2,2,256,256,18]{4,3,5,2,1,0:T(8,128)(2,1)} copy(bf16[2,2,2,256,256,18]{3,2,5,4,1,0:T(2,128)(2,1)} %bitcast.68) | data formatting | bytes 37748736 | tf_op jit(solution)/shard_map/reshape | solution.py:78
  101.1 9.1 %slice.35 = bf16[2,1,2,256,256,18]{3,2,5,4,1,0:T(2,128)(2,1)} slice(bf16[2,2,2,256,256,18]{3,2,5,4,1,0:T(2,128)(2,1)} %bitcast.69), slice={[0:2], [0:1], [0:2], [0:256], [0:256], [0:18]} | slice | bytes 18874368 | tf_op jit(solution)/shard_map/slice | solution.py:84
  110.3 16.7 %broadcast_multiply_fusion.2 = bf16[2,2,2,256,256,18]{4,3,5,2,1,0:T(8,128)(2,1)} fusion(bf16[2,2,2,256,256,18]{4,3,5,2,1,0:T(8,128)(2,1)} %copy.46, bf16[2,2,256]{2,1,0:T(2,128)(2,1)S(1)} %compare_convert_fusion), kind=kLoop, calls=%fused_computation.84 | loop fusion | flops 9437184 | bytes 37750784 | tf_op jit(solution)/shard_map/mul | solution.py:79
  127.0 8.4 %slice_bitcast_fusion = bf16[2,2,256,256,18]{3,2,4,1,0:T(8,128)(2,1)} fusion(bf16[2,2,2,256,256,18]{4,3,5,2,1,0:T(8,128)(2,1)} %broadcast_multiply_fusion.2), kind=kLoop, calls=%fused_computation.83 | loop fusion | bytes 18874368 | tf_op jit(solution)/shard_map/squeeze | solution.py:84
  135.4 29.6 %copy.62 = bf16[2,2,2,256,256,18]{3,5,1,2,0,4:T(8,128)(2,1)} copy(bf16[2,2,2,256,256,18]{4,3,5,2,1,0:T(8,128)(2,1)} %broadcast_multiply_fusion.2) | data formatting | bytes 37748736 | tf_op jit(solution)/shard_map/mul | solution.py:79
  165.1 15.5 %copy.50 = bf16[2,2,256,256,18]{2,4,3,1,0:T(8,128)(2,1)} copy(bf16[2,2,256,256,18]{3,2,4,1,0:T(8,128)(2,1)} %slice_bitcast_fusion) | data formatting | bytes 18874368 | tf_op jit(solution)/shard_map/squeeze | solution.py:84
  180.6 13.3 %fusion.40 = f32[2,2,256,18,18]{4,3,2,1,0:T(8,128)} fusion(bf16[2,2,256,256,18]{2,4,3,1,0:T(8,128)(2,1)} %copy.50, bf16[2,1,2,256,256,18]{3,2,5,4,1,0:T(2,128)(2,1)} %slice.35), kind=kOutput, calls=%fused_computation.80 | convolution fusion | flops 169869312 | bytes 20201472 | tf_op jit(solution)/shard_map/skbai,skbaj->skaij/dot_general | solution.py:83
  193.9 14.0 %copy.51 = f32[2,2,256,18,18]{3,4,2,1,0:T(8,128)} copy(f32[2,2,256,18,18]{4,3,2,1,0:T(8,128)} %fusion.40) | data formatting | bytes 2654208 | tf_op jit(solution)/shard_map/skbai,skbaj->skaij/dot_general | solution.py:83
  207.9 14.1 %fusion.41 = f32[2,1,2,256,18,18]{5,4,3,2,0,1:T(8,128)} fusion(f32[2,2,256,18,18]{4,3,2,1,0:T(8,128)} %fusion.40, f32[2,2,256,18,18]{3,4,2,1,0:T(8,128)} %copy.51), kind=kLoop, calls=%fused_computation.82 | loop fusion | flops 331776 | bytes 3981312 | tf_op jit(solution)/shard_map/stack | solution.py:87
  221.9 11.4 %copy.53 = f32[2,1,2,256,18,18]{3,2,5,4,1,0:T(2,128)S(1)} copy(f32[2,1,2,256,18,18]{5,4,3,2,0,1:T(8,128)} %fusion.41) | data formatting | bytes 2654208 | tf_op jit(solution)/shard_map/stack | solution.py:87
  233.4 21.8 %fusion.42 = f32[2,1,2,256,18,18]{4,5,2,0,3,1:T(8,128)} fusion(bf16[2,2,2,256,256,18]{3,5,1,2,0,4:T(8,128)(2,1)} %copy.62, bf16[2,2,2,256,256,18]{3,2,5,4,1,0:T(2,128)(2,1)} %bitcast.70), kind=kOutput, calls=%fused_computation.85 | convolution fusion | flops 339738624 | bytes 39075840 | tf_op jit(solution)/shard_map/sckbai,sckbaj->skaij/dot_general | solution.py:80
  255.1 11.6 %copy.52 = f32[2,1,2,256,18,18]{3,2,5,4,1,0:T(2,128)S(1)} copy(f32[2,1,2,256,18,18]{4,5,2,0,3,1:T(8,128)} %fusion.42) | data formatting | bytes 2654208 | tf_op jit(solution)/shard_map/stack | solution.py:87
  278.9 60.1 %all-reduce.2.cloned.1.call-done = f32[2,2,256,324]{3,1,2,0:T(2,128)} async-done(((f32[2,2,256,324]{3,1,2,0:T(2,128)}), f32[2,2,256,324]{3,1,2,0:T(2,128)}) %all-reduce.2.cloned.1.call-update) | async-done | bytes 1327120 | tf_op jit(solution)/shard_map/psum | solution.py:93
  346.8 303.3 %while.14 = (s32[]{:T(128)}, f32[64,3]{0,1:T(4,128)}, f32[2,1]{0,1:T(1,128)S(1)}, s32[8]{0:T(128)S(1)}, s32[]{:T(128)}, /*index=5*/f32[64,18]{0,1:T(8,128)S(1)},...) while((s32[]{:T(128)}, f32[64,3]{0,1:T(4,128)}, ...), condition=%wide.region_5.6_spmd.clone, body=%wide.region_4.5_spmd.clone.sunk | while | flops 262103424 | bytes 21960220 | solution.py:59
  361.2 18.2 %convolution_multiply_fusion.3 = f32[13824,64]{0,1:T(8,128)} fusion(f32[18,13824]{1,0:T(8,128)} %mul.712, f32[64,18]{0,1:T(8,128)S(1)} %get-tuple-element.353, f32[13824,64]{0,1:T(8,128)S(1)} %fusion.77, f32[13824]{0:T(1024)S(1)} %get-tuple-element.318, f32[13824]{0:T(1024)S(1)} %get-tuple-element.319), kind=kOutput, calls=%fused_computation.3.clone.1 | convolution fusion | flops 194641920 | bytes 8188416 | tf_op jit(solution)/shard_map/while/body/eval_jaxpr/dot_general | solution.py:42
  399.1 18.2 %convolution_multiply_fusion.3 = f32[13824,64]{0,1:T(8,128)} fusion(f32[18,13824]{1,0:T(8,128)} %mul.712, f32[64,18]{0,1:T(8,128)S(1)} %get-tuple-element.353, f32[13824,64]{0,1:T(8,128)S(1)} %fusion.77, f32[13824]{0:T(1024)S(1)} %get-tuple-element.318, f32[13824]{0:T(1024)S(1)} %get-tuple-element.319), kind=kOutput, calls=%fused_computation.3.clone.1 | convolution fusion | flops 194641920 | bytes 8188416 | tf_op jit(solution)/shard_map/while/body/eval_jaxpr/dot_general | solution.py:42
  436.9 18.2 %convolution_multiply_fusion.3 = f32[13824,64]{0,1:T(8,128)} fusion(f32[18,13824]{1,0:T(8,128)} %mul.712, f32[64,18]{0,1:T(8,128)S(1)} %get-tuple-element.353, f32[13824,64]{0,1:T(8,128)S(1)} %fusion.77, f32[13824]{0:T(1024)S(1)} %get-tuple-element.318, f32[13824]{0:T(1024)S(1)} %get-tuple-element.319), kind=kOutput, calls=%fused_computation.3.clone.1 | convolution fusion | flops 194641920 | bytes 8188416 | tf_op jit(solution)/shard_map/while/body/eval_jaxpr/dot_general | solution.py:42
  474.8 18.2 %convolution_multiply_fusion.3 = f32[13824,64]{0,1:T(8,128)} fusion(f32[18,13824]{1,0:T(8,128)} %mul.712, f32[64,18]{0,1:T(8,128)S(1)} %get-tuple-element.353, f32[13824,64]{0,1:T(8,128)S(1)} %fusion.77, f32[13824]{0:T(1024)S(1)} %get-tuple-element.318, f32[13824]{0:T(1024)S(1)} %get-tuple-element.319), kind=kOutput, calls=%fused_computation.3.clone.1 | convolution fusion | flops 194641920 | bytes 8188416 | tf_op jit(solution)/shard_map/while/body/eval_jaxpr/dot_general | solution.py:42
  512.7 18.2 %convolution_multiply_fusion.3 = f32[13824,64]{0,1:T(8,128)} fusion(f32[18,13824]{1,0:T(8,128)} %mul.712, f32[64,18]{0,1:T(8,128)S(1)} %get-tuple-element.353, f32[13824,64]{0,1:T(8,128)S(1)} %fusion.77, f32[13824]{0:T(1024)S(1)} %get-tuple-element.318, f32[13824]{0:T(1024)S(1)} %get-tuple-element.319), kind=kOutput, calls=%fused_computation.3.clone.1 | convolution fusion | flops 194641920 | bytes 8188416 | tf_op jit(solution)/shard_map/while/body/eval_jaxpr/dot_general | solution.py:42
  550.6 18.2 %convolution_multiply_fusion.3 = f32[13824,64]{0,1:T(8,128)} fusion(f32[18,13824]{1,0:T(8,128)} %mul.712, f32[64,18]{0,1:T(8,128)S(1)} %get-tuple-element.353, f32[13824,64]{0,1:T(8,128)S(1)} %fusion.77, f32[13824]{0:T(1024)S(1)} %get-tuple-element.318, f32[13824]{0:T(1024)S(1)} %get-tuple-element.319), kind=kOutput, calls=%fused_computation.3.clone.1 | convolution fusion | flops 194641920 | bytes 8188416 | tf_op jit(solution)/shard_map/while/body/eval_jaxpr/dot_general | solution.py:42
  568.8 5.5 convolution_add_fusion.2
  588.5 18.2 %convolution_multiply_fusion.3 = f32[13824,64]{0,1:T(8,128)} fusion(f32[18,13824]{1,0:T(8,128)} %mul.712, f32[64,18]{0,1:T(8,128)S(1)} %get-tuple-element.353, f32[13824,64]{0,1:T(8,128)S(1)} %fusion.77, f32[13824]{0:T(1024)S(1)} %get-tuple-element.318, f32[13824]{0:T(1024)S(1)} %get-tuple-element.319), kind=kOutput, calls=%fused_computation.3.clone.1 | convolution fusion | flops 194641920 | bytes 8188416 | tf_op jit(solution)/shard_map/while/body/eval_jaxpr/dot_general | solution.py:42
  626.4 18.2 %convolution_multiply_fusion.3 = f32[13824,64]{0,1:T(8,128)} fusion(f32[18,13824]{1,0:T(8,128)} %mul.712, f32[64,18]{0,1:T(8,128)S(1)} %get-tuple-element.353, f32[13824,64]{0,1:T(8,128)S(1)} %fusion.77, f32[13824]{0:T(1024)S(1)} %get-tuple-element.318, f32[13824]{0:T(1024)S(1)} %get-tuple-element.319), kind=kOutput, calls=%fused_computation.3.clone.1 | convolution fusion | flops 194641920 | bytes 8188416 | tf_op jit(solution)/shard_map/while/body/eval_jaxpr/dot_general | solution.py:42
  (299 shorter events, 173.6 us)
Async XLA Ops:
  8.0 267.3 %copy-start = (s32[512]{0:T(512)S(1)}, s32[512]{0:T(512)}, u32[]{:S(2)}) copy-start(s32[512]{0:T(512)} %param.15) | copy-start | bytes 6148
  8.0 266.3 %sort.19.cloned.1.call-start = ((), (), s32[]{:S(2)}) async-start(), calls=%async_computation.1 | async-start | bytes 12320 | tf_op jit(solution)/shard_map/jit(argsort)/sort | solution.py:91
  9.9 329.0 %all-reduce.2.cloned.1.call-start = ((), (), s32[]{:S(2)}) async-start(), calls=%async_computation | async-start | bytes 3145728 | tf_op jit(solution)/shard_map/psum | solution.py:93
  101.1 9.1 %copy-start.8 = (s32[2,2]{1,0:T(2,128)S(1)}, s32[2,2]{1,0:T(2,128)}, u32[]{:S(2)}) copy-start(s32[2,2]{1,0:T(2,128)} %param.12) | copy-start | bytes 52
  255.1 11.6 %copy-start.9 = (f32[2]{0:T(128)S(1)}, f32[2]{0:T(128)}, u32[]{:S(2)}) copy-start(f32[2]{0:T(128)} %param.13) | copy-start | bytes 28
  347.0 6.4 copy-start.5
  379.4 5.5 copy-start.6
  379.4 5.5 copy-start.12
  384.9 6.4 copy-start.5
  417.3 5.5 copy-start.6
  417.3 5.5 copy-start.12
  422.8 6.4 copy-start.5
  455.2 5.5 copy-start.6
  455.2 5.5 copy-start.12
  460.7 6.4 copy-start.5
  493.0 5.5 copy-start.12
  498.6 6.4 copy-start.5
  530.9 5.5 copy-start.12
  536.5 6.4 copy-start.5
  568.8 5.5 copy-start.12
  574.4 6.4 copy-start.5
  606.7 5.5 copy-start.12
  612.3 6.4 copy-start.5
  644.6 5.5 copy-start.12
  (40 other events, 114.3 us)
Sparse Core Ops, SparseCore 0:
  11.7 2.2 sort.21.cloned.1.call-done
  (1 shorter events, 0.0 us)
Sparse Core Ops, SparseCore 1:
  274.1 64.8 all-reduce.1
where the time goes:
time: 668 us; the launch traced here: 663 us
  matrix products  255 us (38%)
  local copies, waits for them, and re-layouts  234 us (35%)
  other arithmetic  83.3 us (12%)
  waiting for transfers between devices  60.1 us (9%)
  between operations  15.7 us (2%)
  blocking collectives  9.31 us (1%)
    dot_general x8, matrix products, force_block(): smooth = jnp.dot(moments, form_table, precision=highest)  146 us
    psum x1, waiting for transfers between devices, shards(): summed = lax.psum(density_local, ('ka', 'ba'))  60.1 us
    unnamed x19, local copies, waits for them, and re-layouts  47.3 us
    reshape x1, local copies, waits for them, and re-layouts, shards(): coefficients.reshape(spin_count, complex_parts, kcount, bcount, atoms_blk...  45.4 us
    dot_general x8, matrix products, force_block(): return jnp.dot(smooth * wave_term, vectors, precision=highest)  44.3 us
    mul x1, local copies, waits for them, and re-layouts, shards(): masked = values * band_mask[:, None, :, :, None, None]  29.6 us
    dot_general x8, matrix products, force_block(): phases = jnp.dot(places, vectors.T, precision=highest)  29.6 us
    squeeze x2, local copies, waits for them, and re-layouts, shards(): masked[:, 1]  23.9 us
  transfers between devices with their start and end apart: 1, of which 1 were waited for; matrix products, arithmetic and copies ran while one was open for 1% of the time, Pallas kernels for 0%

commit v1 on v0

--- a/solution.py
+++ b/solution.py
@@ -90,7 +90,7 @@
     )
     ranking = jnp.argsort(owner_map.reshape(-1, atoms_blk), axis=1, stable=True)
     own_ranks = lax.dynamic_slice_in_dim(ranking, owner_index * per_owner, per_owner, 1)
-    summed = lax.psum(density_local, ("ka", "ba"))
+    summed = lax.psum(lax.psum(density_local, "ba"), "ka")
     own_rows = lax.dynamic_index_in_dim(own_ranks, group_index, 0, keepdims=False)
     own_density = jnp.take(summed, own_rows, axis=2)
     block_count = own_ranks.shape[0]

time: 668 us -> 698 us (1.045)
  waiting for transfers between devices: 60.1 us -> 90.1 us
    psum x1 -> x2, waiting for transfers between devices: 60.1 us -> 90.1 us  [shards(): summed = lax.psum(lax.psum(density_local, 'ba'), 'ka')]
  transfers between devices with their start and end apart: 1 -> 2, of which waited for: 1 -> 2; matrix products, arithmetic and copies ran while one was open for 1% -> 1% of each run, Pallas kernels for 0% -> 0%
where the time goes in v1:
time: 698 us; the launch traced here: 693 us
  matrix products  255 us (37%)
  local copies, waits for them, and re-layouts  234 us (34%)
  waiting for transfers between devices  90.1 us (13%)
  other arithmetic  83.3 us (12%)
  between operations  15.8 us (2%)
  blocking collectives  9.31 us (1%)
    dot_general x8, matrix products, force_block(): smooth = jnp.dot(moments, form_table, precision=highest)  146 us
    psum x2, waiting for transfers between devices, shards(): summed = lax.psum(lax.psum(density_local, 'ba'), 'ka')  90.1 us
    unnamed x19, local copies, waits for them, and re-layouts  47.3 us
    reshape x1, local copies, waits for them, and re-layouts, shards(): coefficients.reshape(spin_count, complex_parts, kcount, bcount, atoms_blk...  45.4 us
    dot_general x8, matrix products, force_block(): return jnp.dot(smooth * wave_term, vectors, precision=highest)  44.3 us
    mul x1, local copies, waits for them, and re-layouts, shards(): masked = values * band_mask[:, None, :, :, None, None]  29.6 us
    dot_general x8, matrix products, force_block(): phases = jnp.dot(places, vectors.T, precision=highest)  29.6 us
    squeeze x2, local copies, waits for them, and re-layouts, shards(): masked[:, 1]  23.9 us
  transfers between devices with their start and end apart: 2, of which 2 were waited for; matrix products, arithmetic and copies ran while one was open for 1% of the time, Pallas kernels for 0%

profile of v1, /device:TPU:0, one launch (start us, length us, event | category | flops | bytes accessed | tf_op | source)
XLA Modules:
  0.0 693.1 jit_solution(1047650428505457892)
XLA Ops:
  10.0 45.7 %copy.45 = bf16[2,2,2,256,4608]{3,2,4,1,0:T(2,128)(2,1)} copy(bf16[2,2,2,256,4608]{4,3,2,1,0:T(8,128)(2,1)} %param.11) | data formatting | bytes 37748736 | tf_op args[0]
  55.7 45.4 %copy.46 = bf16[2,2,2,256,256,18]{4,3,5,2,1,0:T(8,128)(2,1)} copy(bf16[2,2,2,256,256,18]{3,2,5,4,1,0:T(2,128)(2,1)} %bitcast.68) | data formatting | bytes 37748736 | tf_op jit(solution)/shard_map/reshape | solution.py:78
  101.1 9.1 %slice.35 = bf16[2,1,2,256,256,18]{3,2,5,4,1,0:T(2,128)(2,1)} slice(bf16[2,2,2,256,256,18]{3,2,5,4,1,0:T(2,128)(2,1)} %bitcast.69), slice={[0:2], [0:1], [0:2], [0:256], [0:256], [0:18]} | slice | bytes 18874368 | tf_op jit(solution)/shard_map/slice | solution.py:84
  110.3 16.7 %broadcast_multiply_fusion.2 = bf16[2,2,2,256,256,18]{4,3,5,2,1,0:T(8,128)(2,1)} fusion(bf16[2,2,2,256,256,18]{4,3,5,2,1,0:T(8,128)(2,1)} %copy.46, bf16[2,2,256]{2,1,0:T(2,128)(2,1)S(1)} %compare_convert_fusion), kind=kLoop, calls=%fused_computation.84 | loop fusion | flops 9437184 | bytes 37750784 | tf_op jit(solution)/shard_map/mul | solution.py:79
  127.0 8.4 %slice_bitcast_fusion = bf16[2,2,256,256,18]{3,2,4,1,0:T(8,128)(2,1)} fusion(bf16[2,2,2,256,256,18]{4,3,5,2,1,0:T(8,128)(2,1)} %broadcast_multiply_fusion.2), kind=kLoop, calls=%fused_computation.83 | loop fusion | bytes 18874368 | tf_op jit(solution)/shard_map/squeeze | solution.py:84
  135.4 29.6 %copy.62 = bf16[2,2,2,256,256,18]{3,5,1,2,0,4:T(8,128)(2,1)} copy(bf16[2,2,2,256,256,18]{4,3,5,2,1,0:T(8,128)(2,1)} %broadcast_multiply_fusion.2) | data formatting | bytes 37748736 | tf_op jit(solution)/shard_map/mul | solution.py:79
  165.1 15.5 %copy.50 = bf16[2,2,256,256,18]{2,4,3,1,0:T(8,128)(2,1)} copy(bf16[2,2,256,256,18]{3,2,4,1,0:T(8,128)(2,1)} %slice_bitcast_fusion) | data formatting | bytes 18874368 | tf_op jit(solution)/shard_map/squeeze | solution.py:84
  180.6 13.3 %fusion.40 = f32[2,2,256,18,18]{4,3,2,1,0:T(8,128)} fusion(bf16[2,2,256,256,18]{2,4,3,1,0:T(8,128)(2,1)} %copy.50, bf16[2,1,2,256,256,18]{3,2,5,4,1,0:T(2,128)(2,1)} %slice.35), kind=kOutput, calls=%fused_computation.80 | convolution fusion | flops 169869312 | bytes 20201472 | tf_op jit(solution)/shard_map/skbai,skbaj->skaij/dot_general | solution.py:83
  193.9 14.0 %copy.51 = f32[2,2,256,18,18]{3,4,2,1,0:T(8,128)} copy(f32[2,2,256,18,18]{4,3,2,1,0:T(8,128)} %fusion.40) | data formatting | bytes 2654208 | tf_op jit(solution)/shard_map/skbai,skbaj->skaij/dot_general | solution.py:83
  207.9 14.1 %fusion.41 = f32[2,1,2,256,18,18]{5,4,3,2,0,1:T(8,128)} fusion(f32[2,2,256,18,18]{4,3,2,1,0:T(8,128)} %fusion.40, f32[2,2,256,18,18]{3,4,2,1,0:T(8,128)} %copy.51), kind=kLoop, calls=%fused_computation.82 | loop fusion | flops 331776 | bytes 3981312 | tf_op jit(solution)/shard_map/stack | solution.py:87
  221.9 11.4 %copy.53 = f32[2,1,2,256,18,18]{3,2,5,4,1,0:T(2,128)S(1)} copy(f32[2,1,2,256,18,18]{5,4,3,2,0,1:T(8,128)} %fusion.41) | data formatting | bytes 2654208 | tf_op jit(solution)/shard_map/stack | solution.py:87
  233.4 21.8 %fusion.42 = f32[2,1,2,256,18,18]{4,5,2,0,3,1:T(8,128)} fusion(bf16[2,2,2,256,256,18]{3,5,1,2,0,4:T(8,128)(2,1)} %copy.62, bf16[2,2,2,256,256,18]{3,2,5,4,1,0:T(2,128)(2,1)} %bitcast.70), kind=kOutput, calls=%fused_computation.85 | convolution fusion | flops 339738624 | bytes 39075840 | tf_op jit(solution)/shard_map/sckbai,sckbaj->skaij/dot_general | solution.py:80
  255.1 11.6 %copy.52 = f32[2,1,2,256,18,18]{3,2,5,4,1,0:T(2,128)S(1)} copy(f32[2,1,2,256,18,18]{4,5,2,0,3,1:T(8,128)} %fusion.42) | data formatting | bytes 2654208 | tf_op jit(solution)/shard_map/stack | solution.py:87
  276.1 20.8 %all-reduce.3.cloned.1.call-done = f32[2,2,256,324]{3,1,2,0:T(2,128)} async-done(((f32[2,2,256,324]{3,1,2,0:T(2,128)}), f32[2,2,256,324]{3,1,2,0:T(2,128)}) %all-reduce.3.cloned.1.call-update) | async-done | bytes 1327120 | tf_op jit(solution)/shard_map/psum | solution.py:93
  299.8 69.3 %all-reduce.5.cloned.1.call-done = f32[2,2,256,324]{3,1,2,0:T(2,128)} async-done(((f32[2,2,256,324]{3,1,2,0:T(2,128)}), f32[2,2,256,324]{3,1,2,0:T(2,128)}) %all-reduce.5.cloned.1.call-update) | async-done | bytes 1327120 | tf_op jit(solution)/shard_map/psum | solution.py:93
  376.9 303.2 %while.14 = (s32[]{:T(128)}, f32[64,3]{0,1:T(4,128)}, f32[2,1]{0,1:T(1,128)S(1)}, s32[8]{0:T(128)S(1)}, s32[]{:T(128)}, /*index=5*/f32[64,18]{0,1:T(8,128)S(1)},...) while((s32[]{:T(128)}, f32[64,3]{0,1:T(4,128)}, ...), condition=%wide.region_6.7_spmd.clone, body=%wide.region_5.6_spmd.clone.sunk | while | flops 262103424 | bytes 21960220 | solution.py:59
  391.2 18.2 %convolution_multiply_fusion.3 = f32[13824,64]{0,1:T(8,128)} fusion(f32[18,13824]{1,0:T(8,128)} %mul.712, f32[64,18]{0,1:T(8,128)S(1)} %get-tuple-element.353, f32[13824,64]{0,1:T(8,128)S(1)} %fusion.77, f32[13824]{0:T(1024)S(1)} %get-tuple-element.318, f32[13824]{0:T(1024)S(1)} %get-tuple-element.319), kind=kOutput, calls=%fused_computation.3.clone.1 | convolution fusion | flops 194641920 | bytes 8188416 | tf_op jit(solution)/shard_map/while/body/eval_jaxpr/dot_general | solution.py:42
  429.1 18.2 %convolution_multiply_fusion.3 = f32[13824,64]{0,1:T(8,128)} fusion(f32[18,13824]{1,0:T(8,128)} %mul.712, f32[64,18]{0,1:T(8,128)S(1)} %get-tuple-element.353, f32[13824,64]{0,1:T(8,128)S(1)} %fusion.77, f32[13824]{0:T(1024)S(1)} %get-tuple-element.318, f32[13824]{0:T(1024)S(1)} %get-tuple-element.319), kind=kOutput, calls=%fused_computation.3.clone.1 | convolution fusion | flops 194641920 | bytes 8188416 | tf_op jit(solution)/shard_map/while/body/eval_jaxpr/dot_general | solution.py:42
  467.0 18.2 %convolution_multiply_fusion.3 = f32[13824,64]{0,1:T(8,128)} fusion(f32[18,13824]{1,0:T(8,128)} %mul.712, f32[64,18]{0,1:T(8,128)S(1)} %get-tuple-element.353, f32[13824,64]{0,1:T(8,128)S(1)} %fusion.77, f32[13824]{0:T(1024)S(1)} %get-tuple-element.318, f32[13824]{0:T(1024)S(1)} %get-tuple-element.319), kind=kOutput, calls=%fused_computation.3.clone.1 | convolution fusion | flops 194641920 | bytes 8188416 | tf_op jit(solution)/shard_map/while/body/eval_jaxpr/dot_general | solution.py:42
  504.9 18.2 %convolution_multiply_fusion.3 = f32[13824,64]{0,1:T(8,128)} fusion(f32[18,13824]{1,0:T(8,128)} %mul.712, f32[64,18]{0,1:T(8,128)S(1)} %get-tuple-element.353, f32[13824,64]{0,1:T(8,128)S(1)} %fusion.77, f32[13824]{0:T(1024)S(1)} %get-tuple-element.318, f32[13824]{0:T(1024)S(1)} %get-tuple-element.319), kind=kOutput, calls=%fused_computation.3.clone.1 | convolution fusion | flops 194641920 | bytes 8188416 | tf_op jit(solution)/shard_map/while/body/eval_jaxpr/dot_general | solution.py:42
  542.8 18.2 %convolution_multiply_fusion.3 = f32[13824,64]{0,1:T(8,128)} fusion(f32[18,13824]{1,0:T(8,128)} %mul.712, f32[64,18]{0,1:T(8,128)S(1)} %get-tuple-element.353, f32[13824,64]{0,1:T(8,128)S(1)} %fusion.77, f32[13824]{0:T(1024)S(1)} %get-tuple-element.318, f32[13824]{0:T(1024)S(1)} %get-tuple-element.319), kind=kOutput, calls=%fused_computation.3.clone.1 | convolution fusion | flops 194641920 | bytes 8188416 | tf_op jit(solution)/shard_map/while/body/eval_jaxpr/dot_general | solution.py:42
  580.6 18.2 %convolution_multiply_fusion.3 = f32[13824,64]{0,1:T(8,128)} fusion(f32[18,13824]{1,0:T(8,128)} %mul.712, f32[64,18]{0,1:T(8,128)S(1)} %get-tuple-element.353, f32[13824,64]{0,1:T(8,128)S(1)} %fusion.77, f32[13824]{0:T(1024)S(1)} %get-tuple-element.318, f32[13824]{0:T(1024)S(1)} %get-tuple-element.319), kind=kOutput, calls=%fused_computation.3.clone.1 | convolution fusion | flops 194641920 | bytes 8188416 | tf_op jit(solution)/shard_map/while/body/eval_jaxpr/dot_general | solution.py:42
  618.5 18.2 %convolution_multiply_fusion.3 = f32[13824,64]{0,1:T(8,128)} fusion(f32[18,13824]{1,0:T(8,128)} %mul.712, f32[64,18]{0,1:T(8,128)S(1)} %get-tuple-element.353, f32[13824,64]{0,1:T(8,128)S(1)} %fusion.77, f32[13824]{0:T(1024)S(1)} %get-tuple-element.318, f32[13824]{0:T(1024)S(1)} %get-tuple-element.319), kind=kOutput, calls=%fused_computation.3.clone.1 | convolution fusion | flops 194641920 | bytes 8188416 | tf_op jit(solution)/shard_map/while/body/eval_jaxpr/dot_general | solution.py:42
  656.4 18.2 %convolution_multiply_fusion.3 = f32[13824,64]{0,1:T(8,128)} fusion(f32[18,13824]{1,0:T(8,128)} %mul.712, f32[64,18]{0,1:T(8,128)S(1)} %get-tuple-element.353, f32[13824,64]{0,1:T(8,128)S(1)} %fusion.77, f32[13824]{0:T(1024)S(1)} %get-tuple-element.318, f32[13824]{0:T(1024)S(1)} %get-tuple-element.319), kind=kOutput, calls=%fused_computation.3.clone.1 | convolution fusion | flops 194641920 | bytes 8188416 | tf_op jit(solution)/shard_map/while/body/eval_jaxpr/dot_general | solution.py:42
  (302 shorter events, 179.2 us)
Async XLA Ops:
  8.0 267.3 %copy-start = (s32[512]{0:T(512)S(1)}, s32[512]{0:T(512)}, u32[]{:S(2)}) copy-start(s32[512]{0:T(512)} %param.15) | copy-start | bytes 6148
  8.0 266.4 %sort.19.cloned.1.call-start = ((), (), s32[]{:S(2)}) async-start(), calls=%async_computation.2 | async-start | bytes 12320 | tf_op jit(solution)/shard_map/jit(argsort)/sort | solution.py:91
  9.9 286.9 %all-reduce.3.cloned.1.call-start = ((), (), s32[]{:S(2)}) async-start(), calls=%async_computation | async-start | bytes 3145728 | tf_op jit(solution)/shard_map/psum | solution.py:93
  101.1 9.1 %copy-start.8 = (s32[2,2]{1,0:T(2,128)S(1)}, s32[2,2]{1,0:T(2,128)}, u32[]{:S(2)}) copy-start(s32[2,2]{1,0:T(2,128)} %param.12) | copy-start | bytes 52
  255.1 11.6 %copy-start.9 = (f32[2]{0:T(128)S(1)}, f32[2]{0:T(128)}, u32[]{:S(2)}) copy-start(f32[2]{0:T(128)} %param.13) | copy-start | bytes 28
  274.1 95.0 %all-reduce.5.cloned.1.call-start = ((), (), s32[]{:S(2)}) async-start(), calls=%async_computation.1 | async-start | bytes 3145728 | tf_op jit(solution)/shard_map/psum | solution.py:93
  377.1 7.8 %copy-start.5 = (f32[2,1]{0,1:T(1,128)}, f32[2,1]{0,1:T(1,128)S(1)}, u32[]{:S(2)}) copy-start(f32[2,1]{0,1:T(1,128)S(1)} %get-tuple-element.350) | copy-start | bytes 28 | tf_op jit(solution)/shard_map/while
  377.1 7.8 %copy-start.11 = (s32[8]{0:T(128)}, s32[8]{0:T(128)S(1)}, u32[]{:S(2)}) copy-start(s32[8]{0:T(128)S(1)} %get-tuple-element.351) | copy-start | bytes 100 | tf_op jit(solution)/shard_map/while
  409.5 5.5 copy-start.12
  415.0 7.8 %copy-start.5 = (f32[2,1]{0,1:T(1,128)}, f32[2,1]{0,1:T(1,128)S(1)}, u32[]{:S(2)}) copy-start(f32[2,1]{0,1:T(1,128)S(1)} %get-tuple-element.350) | copy-start | bytes 28 | tf_op jit(solution)/shard_map/while
  415.0 7.8 %copy-start.11 = (s32[8]{0:T(128)}, s32[8]{0:T(128)S(1)}, u32[]{:S(2)}) copy-start(s32[8]{0:T(128)S(1)} %get-tuple-element.351) | copy-start | bytes 100 | tf_op jit(solution)/shard_map/while
  452.9 7.8 %copy-start.5 = (f32[2,1]{0,1:T(1,128)}, f32[2,1]{0,1:T(1,128)S(1)}, u32[]{:S(2)}) copy-start(f32[2,1]{0,1:T(1,128)S(1)} %get-tuple-element.350) | copy-start | bytes 28 | tf_op jit(solution)/shard_map/while
  452.9 7.8 %copy-start.11 = (s32[8]{0:T(128)}, s32[8]{0:T(128)S(1)}, u32[]{:S(2)}) copy-start(s32[8]{0:T(128)S(1)} %get-tuple-element.351) | copy-start | bytes 100 | tf_op jit(solution)/shard_map/while
  485.2 5.5 copy-start.12
  490.8 7.8 %copy-start.5 = (f32[2,1]{0,1:T(1,128)}, f32[2,1]{0,1:T(1,128)S(1)}, u32[]{:S(2)}) copy-start(f32[2,1]{0,1:T(1,128)S(1)} %get-tuple-element.350) | copy-start | bytes 28 | tf_op jit(solution)/shard_map/while
  490.8 7.8 %copy-start.11 = (s32[8]{0:T(128)}, s32[8]{0:T(128)S(1)}, u32[]{:S(2)}) copy-start(s32[8]{0:T(128)S(1)} %get-tuple-element.351) | copy-start | bytes 100 | tf_op jit(solution)/shard_map/while
  528.6 7.8 %copy-start.5 = (f32[2,1]{0,1:T(1,128)}, f32[2,1]{0,1:T(1,128)S(1)}, u32[]{:S(2)}) copy-start(f32[2,1]{0,1:T(1,128)S(1)} %get-tuple-element.350) | copy-start | bytes 28 | tf_op jit(solution)/shard_map/while
  528.6 7.8 %copy-start.11 = (s32[8]{0:T(128)}, s32[8]{0:T(128)S(1)}, u32[]{:S(2)}) copy-start(s32[8]{0:T(128)S(1)} %get-tuple-element.351) | copy-start | bytes 100 | tf_op jit(solution)/shard_map/while
  566.5 7.8 %copy-start.5 = (f32[2,1]{0,1:T(1,128)}, f32[2,1]{0,1:T(1,128)S(1)}, u32[]{:S(2)}) copy-start(f32[2,1]{0,1:T(1,128)S(1)} %get-tuple-element.350) | copy-start | bytes 28 | tf_op jit(solution)/shard_map/while
  566.5 7.8 %copy-start.11 = (s32[8]{0:T(128)}, s32[8]{0:T(128)S(1)}, u32[]{:S(2)}) copy-start(s32[8]{0:T(128)S(1)} %get-tuple-element.351) | copy-start | bytes 100 | tf_op jit(solution)/shard_map/while
  604.4 7.8 %copy-start.5 = (f32[2,1]{0,1:T(1,128)}, f32[2,1]{0,1:T(1,128)S(1)}, u32[]{:S(2)}) copy-start(f32[2,1]{0,1:T(1,128)S(1)} %get-tuple-element.350) | copy-start | bytes 28 | tf_op jit(solution)/shard_map/while
  604.4 7.8 %copy-start.11 = (s32[8]{0:T(128)}, s32[8]{0:T(128)S(1)}, u32[]{:S(2)}) copy-start(s32[8]{0:T(128)S(1)} %get-tuple-element.351) | copy-start | bytes 100 | tf_op jit(solution)/shard_map/while
  642.3 7.8 %copy-start.5 = (f32[2,1]{0,1:T(1,128)}, f32[2,1]{0,1:T(1,128)S(1)}, u32[]{:S(2)}) copy-start(f32[2,1]{0,1:T(1,128)S(1)} %get-tuple-element.350) | copy-start | bytes 28 | tf_op jit(solution)/shard_map/while
  642.3 7.8 %copy-start.11 = (s32[8]{0:T(128)}, s32[8]{0:T(128)S(1)}, u32[]{:S(2)}) copy-start(s32[8]{0:T(128)S(1)} %get-tuple-element.351) | copy-start | bytes 100 | tf_op jit(solution)/shard_map/while
  (41 other events, 155.2 us)
Sparse Core Ops, SparseCore 0:
  11.7 2.2 sort.21.cloned.1.call-done
  (1 shorter events, 0.0 us)
Sparse Core Ops, SparseCore 1:
  274.1 22.7 all-reduce.2
  299.1 69.9 all-reduce.4
